TPU v7x, 256 devices: a whole 4x4x8 slice. The times are simulated.
256 devices in a mesh: seg: 4 (over y_hi, core), mic: 64 (over z, x, y_lo).
Axes of the slice: x: 4, y: 4 (y_hi: 2, y_lo: 2; y = y_hi * 2 + y_lo), z: 8, core: 2. Of those that a mesh axis runs over, the one named last changes fastest.
Arguments:
- time_data: bfloat16 [128, 4096, 1024], P('seg', 'mic'), may hold values from -6 to 6
- order_bin: int32 [1], replicated, may hold values from 32 to 203
- mic_pos: int32 [3, 4096], replicated, may hold values from -2000 to 2000
- grid_pos: int32 [3, 131072], P(None, 'mic'), may hold values from -1500 to 1500
Outputs:
- beam_power: float32 [64, 2048], P('mic', 'seg')
All inputs are finite; a program needn't handle non-finite values.
Results may differ from a plain program's by a relative error of at most 0.00083.
Values may be sent and summed in bfloat16 or wider, within the bound.
A program may use at most 256 MiB of HBM per device.

v0:
```python
import math
import jax
import jax.numpy as jnp
from jax import lax
from jax.sharding import PartitionSpec as P


def spectral_table(order_value, samples):
    times = jnp.arange(samples, dtype=jnp.int32)
    turned = order_value * times % samples
    angle = turned.astype(jnp.float32) * (2.0 * math.pi / samples)
    window = 0.5 - 0.5 * jnp.cos(times.astype(jnp.float32) * (2.0 * math.pi / samples))
    return jnp.stack([window * jnp.cos(angle), -(window * jnp.sin(angle))]).astype(jnp.bfloat16)


def stacked_left(spectra):
    real_part = spectra[0]
    imag_part = spectra[1]
    upper = jnp.concatenate([real_part, -imag_part], axis=1)
    lower = jnp.concatenate([imag_part, real_part], axis=1)
    return jnp.concatenate([upper, lower], axis=0)


def beam_block(left, mic_part, points, wave):
    offsets = (points[:, None, :] - mic_part[:, :, None]).astype(jnp.float32) * 0.001
    distance = jnp.sqrt(offsets[0] * offsets[0] + offsets[1] * offsets[1] + offsets[2] * offsets[2])
    phase = wave * distance
    steering = jnp.concatenate([jnp.cos(phase), jnp.sin(phase)], axis=0).astype(jnp.bfloat16)
    return jnp.dot(left, steering, preferred_element_type=jnp.float32)


def make_folder(points, mic_pos, wave):

    def accumulate(carry, piece, start):
        left = stacked_left(piece)
        return beam_block(left, mic_pos, points, wave)

    return accumulate


def shards(time_data, order_bin, mic_pos, grid_pos):
    seg_dev = time_data.shape[0]
    mic_dev = time_data.shape[1]
    samples = time_data.shape[2]
    table = spectral_table(order_bin[0], samples)
    rows = time_data.reshape(seg_dev * mic_dev, samples)
    spec = jnp.dot(rows, table.T, preferred_element_type=jnp.float32)
    spectra = spec.T.reshape(2, seg_dev, mic_dev).astype(jnp.bfloat16)
    wave = (
        order_bin[0].astype(jnp.float32)
        * jnp.float32(2.0 * math.pi * 51200.0 / 343.0)
        / jnp.float32(samples)
    )
    seg_count = lax.axis_size("seg")
    seg_total = seg_count * seg_dev
    mic_total = lax.axis_size("mic") * mic_dev
    denom = jnp.float32(seg_total * mic_total * 0.375 * samples)
    slab_width = grid_pos.shape[1]
    own_width = slab_width // seg_count
    folder = make_folder(grid_pos, mic_pos, wave)
    empty = jnp.zeros((2 * seg_dev, slab_width), jnp.float32)
    beams = folder(empty, lax.all_gather(spectra, "mic", axis=2, tiled=True), jnp.int32(0))
    partial_power = jnp.sum(beams * beams, axis=0) / denom
    beam_power = lax.psum_scatter(partial_power, "seg", scatter_dimension=0, tiled=True)
    return beam_power.reshape(1, own_width)


def solution(mesh):
    placed = (P("seg", "mic", None), P(), P(), P(None, "mic"))
    return jax.shard_map(
        shards, mesh=mesh, in_specs=placed, out_specs=P("mic", "seg"), check_vma=False
    )
```

profile of v0, /device:TPU:1, one launch (start us, length us, event | category | flops | bytes accessed | tf_op | source)
XLA Modules:
  0.0 471.5 jit_solution(192973803990093008)
XLA Ops:
  0.0 32.1 %convert_multiply_fusion = f32[3,4096,2048]{2,1,0:T(8,128)} fusion(s32[3,4096]{1,0:T(4,128)} %param.6, s32[3,2048]{1,0:T(4,128)} %param.7), kind=kLoop, calls=%fused_computation | loop fusion | flops 75497472 | bytes 100737024 | tf_op jit(solution)/shard_map/mul | solution.py:25
  32.8 124.3 %fusion.8 = (bf16[4096,2048]{1,0:T(8,128)(2,1)}, f32[1,4096,2048]{2,1,0:T(8,128)S(1)}) fusion(f32[3,4096,2048]{2,1,0:T(8,128)} %convert_multiply_fusion, f32[]{:T(128)S(6)} %div.9), kind=kLoop, calls=%fused_computation.14 | loop fusion | flops 58720256 | bytes 150994944 | tf_op jit(solution)/shard_map/convert
  157.1 0.0 copy-start
  157.1 108.2 %fusion.9 = bf16[4096,2048]{1,0:T(8,128)(2,1)} fusion(f32[1,4096,2048]{2,1,0:T(8,128)S(1)} %get-tuple-element.6), kind=kLoop, calls=%fused_computation.15 | loop fusion | flops 8388608 | bytes 50331648 | tf_op jit(solution)/shard_map/convert.1
  265.3 0.3 negate_convert_fusion
  265.5 0.0 copy-done
  265.5 1.7 convolution_convert_fusion
  267.3 0.1 copy.6
  267.4 144.7 %all_gather.3 = bf16[2,32,4096]{1,0,2:T(2,128)(2,1)S(1)} all-gather(bf16[2,32,64]{1,0,2:T(2,128)(2,1)S(1)} %copy.6), channel_id=1, replica_groups=mesh['seg'=4,'mic'=64] {'mic'}, dimensions={2}, use_global_device_ids=true | all-gather | bytes 532480 | tf_op jit(solution)/shard_map/all_gather | solution.py:62
  412.1 3.8 fusion.31
  415.9 0.0 copy-start.1
  415.9 4.5 copy.9
  420.4 2.1 copy.10
  422.5 12.7 %fusion.13 = f32[2048]{0:T(1024)S(1)} fusion(bf16[4096,2048]{1,0:T(8,128)(2,1)} %fusion.9, bf16[4096,2048]{1,0:T(8,128)(2,1)} %get-tuple-element.5, bf16[32,4096]{1,0:T(8,128)(2,1)S(1)} %bitcast.17, bf16[32,4096]{1,0:T(8,128)(2,1)S(1)} %bitcast.16, bf16[32,4096]{1,0:T(8,128)(2,1)S(1)} %bitcast_negate_fusion), kind=kOutput, calls=%fused_computation.17 | convolution fusion | flops 2219046912 | bytes 34349056 | tf_op jit(solution)/shard_map/dot_general | solution.py:29
  435.3 34.3 %all-reduce = f32[2048]{0:T(1024)S(1)} all-reduce(f32[2048]{0:T(1024)S(1)} %broadcast_multiply_fusion), channel_id=2, replica_groups=mesh['seg'=4,'mic'=64] {'seg'}, use_global_device_ids=true, to_apply=%region_1.2.clone | all-reduce | flops 2048 | bytes 16384
  469.6 0.0 copy-done.1
  469.6 0.6 dynamic-slice
  470.9 0.7 dynamic-slice.1
  (2 shorter events, 0.0 us)
Async XLA Ops:
  157.1 108.5 %copy-start = (bf16[32,64,1024]{2,1,0:T(8,128)(2,1)S(1)}, bf16[32,64,1024]{2,1,0:T(8,128)(2,1)}, u32[]{:S(2)}) copy-start(bf16[32,64,1024]{2,1,0:T(8,128)(2,1)} %param.4) | copy-start | bytes 12582916
  415.9 53.7 %copy-start.1 = (u32[256]{0:T(256)S(1)}, u32[256]{0:T(256)}, u32[]{:S(2)}) copy-start(u32[256]{0:T(256)} %constant.33) | copy-start | bytes 3076
where the time goes:
time: 472 us
  other arithmetic  265 us (56%)
  blocking collectives  179 us (38%)
  matrix products  14.5 us (3%)
  local copies, waits for them, and re-layouts  11.7 us (2%)
    another operation x3, other arithmetic  233 us
    all_gather x1, blocking collectives, shards(): lax.all_gather(spectra, 'mic', axis=2, tiled=True)  145 us
    unnamed x1, blocking collectives  34.3 us
    mul x1, other arithmetic, beam_block(): (points[:, None, :] - mic_part[:, :, None]).astype(jnp.float32) * 0.001  32.1 us
    dot_general x1, matrix products, beam_block(): return jnp.dot(left, steering, preferred_element_type=jnp.float32)  12.7 us

commit v1 on v0

--- a/solution.py
+++ b/solution.py
@@ -59,7 +59,13 @@
     own_width = slab_width // seg_count
     folder = make_folder(grid_pos, mic_pos, wave)
     empty = jnp.zeros((2 * seg_dev, slab_width), jnp.float32)
-    beams = folder(empty, lax.all_gather(spectra, "mic", axis=2, tiled=True), jnp.int32(0))
+    beams = folder(
+        empty,
+        jnp.concatenate(
+            lax.all_to_all(jnp.stack([spectra] * lax.axis_size("mic")), "mic", 0, 0), axis=2
+        ),
+        jnp.int32(0),
+    )
     partial_power = jnp.sum(beams * beams, axis=0) / denom
     beam_power = lax.psum_scatter(partial_power, "seg", scatter_dimension=0, tiled=True)
     return beam_power.reshape(1, own_width)

time: 472 us -> 311 us (0.66)
  blocking collectives: 179 us -> 7.6 us
  starting transfers between devices: 0 us -> 13.7 us
  local copies, waits for them, and re-layouts: 11.7 us -> 5.15 us
    all_gather x1 -> x0, blocking collectives: 145 us -> none  [shards(): lax.all_gather(spectra, 'mic', axis=2, tiled=True)]
    unnamed x1, blocking collectives: 34.3 us -> 7.6 us
    all_to_all x0 -> x1, starting transfers between devices: none -> 13.7 us  [shards(): lax.all_to_all(jnp.stack([spectra] * lax.axis_size('mic')), 'mic', 0, 0)]
  transfers between devices with their start and end apart: 0 -> 1, of which waited for: 0 -> 0; matrix products, arithmetic and copies ran while one was open for 0% -> 86% of each run, Pallas kernels for 0% -> 0%
where the time goes in v1:
time: 311 us; the launch traced here: 309 us
  other arithmetic  265 us (85%)
  matrix products  16.6 us (5%)
  starting transfers between devices  13.7 us (4%)
  blocking collectives  7.6 us (2%)
  local copies, waits for them, and re-layouts  5.15 us (2%)
    another operation x3, other arithmetic  233 us
    mul x1, other arithmetic, beam_block(): (points[:, None, :] - mic_part[:, :, None]).astype(jnp.float32) * 0.001  32.1 us
    all_to_all x1, starting transfers between devices, shards(): lax.all_to_all(jnp.stack([spectra] * lax.axis_size('mic')), 'mic', 0, 0)  13.7 us
    dot_general x1, matrix products, beam_block(): return jnp.dot(left, steering, preferred_element_type=jnp.float32)  12.7 us
    unnamed x1, blocking collectives  7.6 us
  transfers between devices with their start and end apart: 1, of which 0 were waited for; matrix products, arithmetic and copies ran while one was open for 86% of the time, Pallas kernels for 0%

profile of v1, /device:TPU:1, one launch (start us, length us, event | category | flops | bytes accessed | tf_op | source)
XLA Modules:
  0.0 309.4 jit_solution(7771757319805510224)
XLA Ops:
  0.7 0.3 negate_convert_fusion
  0.9 3.9 %convolution_convert_fusion = bf16[2,32,64]{2,0,1:T(2,128)(2,1)S(1)} fusion(bf16[32,64,1024]{2,1,0:T(8,128)(2,1)} %param.4, bf16[1,1024]{1,0:T(2,128)(2,1)S(1)} %get-tuple-element.9, bf16[1,1024]{1,0:T(2,128)(2,1)S(1)} %get-tuple-element.10), kind=kOutput, calls=%fused_computation.18 | convolution fusion | flops 8400896 | bytes 4206592 | tf_op jit(solution)/shard_map/dot_general | solution.py:47
  4.8 0.3 stack.6
  5.1 1.6 reshape.116
  6.7 13.7 %all-to-all-start = ((bf16[64,2,2048]{2,1,0:T(2,128)(2,1)}), bf16[64,2,2048]{2,1,0:T(2,128)(2,1)S(1)}, u32[]{:S(2)}, u32[]{:S(2)}) async-start(bf16[64,2,2048]{2,1,0:T(2,128)(2,1)} %reshape.116), calls=%async_computation | async-start | bytes 1048576 | tf_op jit(solution)/shard_map/all_to_all | solution.py:65
  20.4 32.1 %convert_multiply_fusion = f32[3,4096,2048]{2,1,0:T(8,128)} fusion(s32[3,4096]{1,0:T(4,128)} %param.6, s32[3,2048]{1,0:T(4,128)} %param.7), kind=kLoop, calls=%fused_computation | loop fusion | flops 75497472 | bytes 100737024 | tf_op jit(solution)/shard_map/mul | solution.py:25
  52.5 124.3 %fusion.8 = (bf16[4096,2048]{1,0:T(8,128)(2,1)}, f32[1,4096,2048]{2,1,0:T(8,128)S(1)}) fusion(f32[3,4096,2048]{2,1,0:T(8,128)} %convert_multiply_fusion, f32[]{:T(128)S(6)} %div.9), kind=kLoop, calls=%fused_computation.14 | loop fusion | flops 58720256 | bytes 150994944 | tf_op jit(solution)/shard_map/convert
  176.8 0.0 copy-start
  176.8 108.2 %fusion.9 = bf16[4096,2048]{1,0:T(8,128)(2,1)} fusion(f32[1,4096,2048]{2,1,0:T(8,128)S(1)} %get-tuple-element.6), kind=kLoop, calls=%fused_computation.15 | loop fusion | flops 8388608 | bytes 50331648 | tf_op jit(solution)/shard_map/convert.1
  285.0 0.0 copy-done
  285.0 0.6 dynamic-slice
  286.2 0.0 all-to-all-done
  286.3 0.7 reshape.117
  286.9 0.1 fusion.31
  287.0 0.2 copy.8
  287.2 0.5 squeeze.7
  287.7 0.2 copy.9
  287.9 0.5 squeeze.8
  288.4 12.7 %fusion.13 = f32[2048]{0:T(1024)S(1)} fusion(bf16[4096,2048]{1,0:T(8,128)(2,1)} %fusion.9, bf16[4096,2048]{1,0:T(8,128)(2,1)} %get-tuple-element.5, bf16[32,4096]{1,0:T(8,128)(2,1)S(1)} %squeeze.7, bf16[32,4096]{1,0:T(8,128)(2,1)S(1)} %squeeze.8, bf16[32,4096]{1,0:T(8,128)(2,1)S(1)} %neg.14), kind=kOutput, calls=%fused_computation.17 | convolution fusion | flops 2219046912 | bytes 34349056 | tf_op jit(solution)/shard_map/dot_general | solution.py:29
  301.2 7.6 %all-reduce = f32[2048]{0:T(1024)S(1)} all-reduce(f32[2048]{0:T(1024)S(1)} %broadcast_multiply_fusion), channel_id=2, replica_groups=mesh['seg'=4,'mic'=64] {'seg'}, use_global_device_ids=true, to_apply=%region_1.2.clone | all-reduce | flops 2048 | bytes 16384
  308.8 0.7 dynamic-slice.1
  (3 shorter events, 0.1 us)
Async XLA Ops:
  6.7 279.6 %all-to-all-start = ((bf16[64,2,2048]{2,1,0:T(2,128)(2,1)}), bf16[64,2,2048]{2,1,0:T(2,128)(2,1)S(1)}, u32[]{:S(2)}, u32[]{:S(2)}) async-start(bf16[64,2,2048]{2,1,0:T(2,128)(2,1)} %reshape.116), calls=%async_computation | async-start | bytes 1048576 | tf_op jit(solution)/shard_map/all_to_all | solution.py:65
  176.8 108.2 %copy-start = (u32[256]{0:T(256)S(1)}, u32[256]{0:T(256)}, u32[]{:S(2)}) copy-start(u32[256]{0:T(256)} %constant.33) | copy-start | bytes 3076
